TPU v7x, 32 devices: a whole 2x2x4 slice. The times are simulated.
32 devices in a mesh: dp: 8 (over z, x), tensor: 4 (over y, core).
Axes of the slice: x: 2, y: 2, z: 4, core: 2. Of those that a mesh axis runs over, the one named last changes fastest.
Arguments:
- layer_in: bfloat16 [32768, 768], P(('dp', 'tensor')), may hold values from -6 to 6
- query_weight: bfloat16 [768, 768], P('dp', 'tensor'), may hold values from -0.3125 to 0.3125
- key_weight: bfloat16 [768, 768], P('dp', 'tensor'), may hold values from -0.3125 to 0.3125
- value_weight: bfloat16 [768, 768], P('dp', 'tensor'), may hold values from -0.21875 to 0.21875
- output_weight: bfloat16 [768, 768], P('tensor', 'dp'), may hold values from -0.875 to 0.875
- inner_weight: bfloat16 [768, 3072], P('dp', 'tensor'), may hold values from -0.21875 to 0.21875
- outer_weight: bfloat16 [3072, 768], P('tensor', 'dp'), may hold values from -0.15625 to 0.15625
- query_bias: float32 [768], P(('dp', 'tensor')), may hold values from -3 to 3
- value_bias: float32 [768], P(('dp', 'tensor')), may hold values from -3 to 3
- output_bias: float32 [768], P(('dp', 'tensor')), may hold values from -3 to 3
- inner_bias: float32 [3072], P(('dp', 'tensor')), may hold values from -3 to 3
- outer_bias: float32 [768], P(('dp', 'tensor')), may hold values from -3 to 3
- first_gain: float32 [768], P(('dp', 'tensor')), may hold values from 0.5 to 1.5
- first_shift: float32 [768], P(('dp', 'tensor')), may hold values from -2 to 2
- second_gain: float32 [768], P(('dp', 'tensor')), may hold values from 0.5 to 1.5
- second_shift: float32 [768], P(('dp', 'tensor')), may hold values from -2 to 2
- segment_ids: int32 [32768], P('dp'), may hold values from 0 to 7, as said below
- pad_mask: int32 [32768], P('dp'), may hold values from 0 to 1, as said below
- random_blocks: int32 [16, 32, 3], P('dp'), may hold values from 0 to 31
- global_blocks: int32 [16, 8, 2], P('dp'), may hold values from 0 to 31, as said below
- output_grad: bfloat16 [32768, 768], P(('dp', 'tensor')), may hold values from -6 to 6
Outputs:
- layer_out: bfloat16 [32768, 768], P(('dp', 'tensor'))
- input_grad: float32 [32768, 768], P(('dp', 'tensor'))
- query_weight_grad: float32 [768, 768], P('dp', 'tensor')
- key_weight_grad: float32 [768, 768], P('dp', 'tensor')
- value_weight_grad: float32 [768, 768], P('dp', 'tensor')
- output_weight_grad: float32 [768, 768], P('tensor', 'dp')
- inner_weight_grad: float32 [768, 3072], P('dp', 'tensor')
- outer_weight_grad: float32 [3072, 768], P('tensor', 'dp')
- query_bias_grad: float32 [768], P(('dp', 'tensor'))
- value_bias_grad: float32 [768], P(('dp', 'tensor'))
- output_bias_grad: float32 [768], P(('dp', 'tensor'))
- inner_bias_grad: float32 [3072], P(('dp', 'tensor'))
- outer_bias_grad: float32 [768], P(('dp', 'tensor'))
- first_gain_grad: float32 [768], P(('dp', 'tensor'))
- first_shift_grad: float32 [768], P(('dp', 'tensor'))
- second_gain_grad: float32 [768], P(('dp', 'tensor'))
- second_shift_grad: float32 [768], P(('dp', 'tensor'))
Inputs may be any that keep to these rules, and one draw needn't show every extreme that they name: `segment_ids`: within each sequence of 2048 tokens the numbers start at 0, never fall and rise by one at each new document; every sequence holds 8 documents; every document but the last of a sequence has 192 tokens or more; padding tokens carry the number of the sequence's last document. `pad_mask`: the padding of a sequence is its last 0 to 127 tokens. `global_blocks`: row s of a sequence holds two block indices for document number s: the first is the block of the document's first token, the second lies one or two blocks after it, or is the last block; the two may be equal.
All inputs are finite; a program needn't handle non-finite values.
Results may differ from a plain program's by a relative error of at most 0.02.
Values may be sent and summed in bfloat16 or wider, within the bound.
A program may use at most 320 MiB of HBM per device.

v0:
```python
from functools import partial

import jax
import jax.numpy as jnp
import numpy as np
from jax import lax
from jax.sharding import PartitionSpec as P

HD = 64


EPSILON = 1e-06
NEGATIVE = -1e30


def entry_rules():
    earlier_same = np.zeros((10, 10), dtype=bool)
    for latter in range(10):
        for former in range(latter):
            if latter < 6 or former < 6 or (latter, former) in ((7, 6), (9, 8)):
                earlier_same[latter, former] = True
    kind_first = np.array([False] * 6 + [True, True, False, False])
    kind_second = np.array([False] * 8 + [True, True])
    plain_kind = np.array([True] * 6 + [False] * 4)
    return (earlier_same, kind_first, kind_second, plain_kind)


def block_layout(seg_row, pad_row, random_row, global_row):
    nblocks = random_row.shape[0]
    block_size = seg_row.shape[0] // nblocks
    earlier_same, kind_first, kind_second, plain_kind = entry_rules()
    seg_blocks = seg_row.reshape(nblocks, block_size)
    pad_blocks = pad_row.reshape(nblocks, block_size)
    first_seg = seg_blocks[:, 0]
    last_seg = seg_blocks[:, -1]
    numbers = jnp.arange(global_row.shape[0], dtype=jnp.int32)
    pick_first = (first_seg[:, None] == numbers[None, :]).astype(jnp.int32)
    pick_last = (last_seg[:, None] == numbers[None, :]).astype(jnp.int32)
    global_first = jnp.sum(pick_first[:, :, None] * global_row[None], axis=1)
    global_last = jnp.sum(pick_last[:, :, None] * global_row[None], axis=1)
    block_ids = jnp.arange(nblocks, dtype=jnp.int32)
    window = jnp.stack([block_ids - 1, block_ids, block_ids + 1], axis=1)
    wanted = jnp.concatenate([window, random_row, global_first, global_last], axis=1)
    inside = (wanted >= 0) & (wanted < nblocks)
    repeated = jnp.any((wanted[:, :, None] == wanted[:, None, :]) & earlier_same[None], axis=2)
    on_first = seg_blocks == first_seg[:, None]
    on_second = (seg_blocks == last_seg[:, None]) & (last_seg != first_seg)[:, None]
    row_ok = (
        plain_kind[None, None, :]
        | kind_first[None, None, :] & on_first[:, :, None]
        | kind_second[None, None, :] & on_second[:, :, None]
    )
    entry_ok = row_ok & (inside & jnp.logical_not(repeated))[:, None, :]
    gather_ids = jnp.clip(wanted, 0, nblocks - 1)
    key_segs = seg_blocks[gather_ids]
    key_pads = pad_blocks[gather_ids]
    same_seg = seg_blocks[:, :, None, None] == key_segs[:, None, :, :]
    self_key = (gather_ids == block_ids[:, None])[:, None, :, None] & jnp.eye(
        block_size, dtype=bool
    )[None, :, None, :]
    allowed = same_seg & ((key_pads == 1)[:, None] | self_key) & entry_ok[:, :, :, None]
    return (gather_ids, allowed)


def block_operands(queries, keys, values, gather_ids, allowed):
    query_count, block_size = (allowed.shape[0], allowed.shape[1])
    key_count = keys.shape[0] // block_size
    heads_here = queries.shape[1] // HD
    query_blocks = queries.reshape(query_count, block_size, heads_here, HD)
    key_blocks = keys.reshape(key_count, block_size, heads_here, HD)[gather_ids]
    value_blocks = values.reshape(key_count, block_size, heads_here, HD)[gather_ids]
    scores = jnp.einsum(
        "iahd,iechd->ihaec", query_blocks, key_blocks, preferred_element_type=jnp.float32
    ) * HD ** (-0.5)
    return (query_blocks, key_blocks, value_blocks, scores)


def attend_forward(item):
    queries, keys, values, gather_ids, allowed = item
    query_blocks, key_blocks, value_blocks, scores = block_operands(
        queries, keys, values, gather_ids, allowed
    )
    masked = jnp.where(allowed[:, None], scores, NEGATIVE)
    highest = jnp.max(masked, axis=(3, 4), keepdims=True)
    expos = jnp.exp(masked - highest)
    totals = jnp.sum(expos, axis=(3, 4), keepdims=True)
    prob_low = (expos / totals).astype(jnp.bfloat16)
    mixed = jnp.einsum(
        "ihaec,iechd->iahd", prob_low, value_blocks, preferred_element_type=jnp.float32
    )
    return (mixed.astype(jnp.bfloat16).reshape(queries.shape), highest + jnp.log(totals))


def attend_backward(item):
    queries, keys, values, gather_ids, allowed, grad_mixed, log_totals = item
    query_blocks, key_blocks, value_blocks, scores = block_operands(
        queries, keys, values, gather_ids, allowed
    )
    query_count, block_size, heads_here = (
        query_blocks.shape[0],
        query_blocks.shape[1],
        query_blocks.shape[2],
    )
    key_count = keys.shape[0] // block_size
    prob_full = jnp.exp(jnp.where(allowed[:, None], scores - log_totals, NEGATIVE))
    prob_low = prob_full.astype(jnp.bfloat16)
    grad_blocks = grad_mixed.reshape(query_count, block_size, heads_here, HD)
    grad_probs = jnp.einsum(
        "iahd,iechd->ihaec", grad_blocks, value_blocks, preferred_element_type=jnp.float32
    )
    inner_sum = jnp.sum(grad_probs * prob_full, axis=(3, 4), keepdims=True)
    grad_scores = (prob_full * (grad_probs - inner_sum)).astype(jnp.bfloat16)
    grad_query = jnp.einsum(
        "ihaec,iechd->iahd", grad_scores, key_blocks, preferred_element_type=jnp.float32
    ) * HD ** (-0.5)
    key_parts = jnp.einsum(
        "ihaec,iahd->iechd", grad_scores, query_blocks, preferred_element_type=jnp.float32
    ) * HD ** (-0.5)
    value_parts = jnp.einsum(
        "ihaec,iahd->iechd", prob_low, grad_blocks, preferred_element_type=jnp.float32
    )
    empty = jnp.zeros((key_count, block_size, heads_here, HD), jnp.float32)
    grad_key = empty.at[gather_ids].add(key_parts)
    grad_value = empty.at[gather_ids].add(value_parts)
    return (
        grad_query.reshape(queries.shape),
        grad_key.reshape(keys.shape),
        grad_value.reshape(keys.shape),
    )


def layer_norm(resid, gain, shift):
    center = resid - jnp.mean(resid, axis=1, keepdims=True)
    inverse = lax.rsqrt(jnp.mean(center * center, axis=1, keepdims=True) + EPSILON)
    normal_hat = center * inverse
    return (normal_hat * gain + shift, normal_hat, inverse)


def norm_backward(grad_normed, normal_hat, inverse, gain):
    grad_hat = grad_normed * gain
    grad_resid = inverse * (
        grad_hat
        - jnp.mean(grad_hat, axis=1, keepdims=True)
        - normal_hat * jnp.mean(grad_hat * normal_hat, axis=1, keepdims=True)
    )
    return (grad_resid, jnp.sum(grad_normed * normal_hat, axis=0), jnp.sum(grad_normed, axis=0))


def contract_rows(left, right):
    return lax.dot_general(
        left, right, (((0,), (0,)), ((), ())), preferred_element_type=jnp.float32
    )


def contract_cols(left, right):
    return lax.dot_general(
        left, right, (((1,), (1,)), ((), ())), preferred_element_type=jnp.float32
    )


def on_device(
    layer_in,
    query_weight,
    key_weight,
    value_weight,
    output_weight,
    inner_weight,
    outer_weight,
    query_bias,
    value_bias,
    output_bias,
    inner_bias,
    outer_bias,
    first_gain,
    first_shift,
    second_gain,
    second_shift,
    segment_ids,
    pad_mask,
    random_blocks,
    global_blocks,
    output_grad,
):
    tensor_rank = lax.axis_index("tensor")
    local_rows = layer_in.shape[0]
    query_full, key_full, value_full, inner_full, output_full, outer_full = (
        lax.all_gather(query_weight, "dp", axis=0, tiled=True),
        lax.all_gather(key_weight, "dp", axis=0, tiled=True),
        lax.all_gather(value_weight, "dp", axis=0, tiled=True),
        lax.all_gather(inner_weight, "dp", axis=0, tiled=True),
        lax.all_gather(output_weight, "dp", axis=1, tiled=True),
        lax.all_gather(outer_weight, "dp", axis=1, tiled=True),
    )
    (
        query_bias_all,
        value_bias_all,
        output_bias_all,
        inner_bias_all,
        outer_bias_all,
        first_gain_all,
        first_shift_all,
        second_gain_all,
        second_shift_all,
    ) = (
        lax.all_gather(query_bias, ("dp", "tensor"), axis=0, tiled=True),
        lax.all_gather(value_bias, ("dp", "tensor"), axis=0, tiled=True),
        lax.all_gather(output_bias, ("dp", "tensor"), axis=0, tiled=True),
        lax.all_gather(inner_bias, ("dp", "tensor"), axis=0, tiled=True),
        lax.all_gather(outer_bias, ("dp", "tensor"), axis=0, tiled=True),
        lax.all_gather(first_gain, ("dp", "tensor"), axis=0, tiled=True),
        lax.all_gather(first_shift, ("dp", "tensor"), axis=0, tiled=True),
        lax.all_gather(second_gain, ("dp", "tensor"), axis=0, tiled=True),
        lax.all_gather(second_shift, ("dp", "tensor"), axis=0, tiled=True),
    )
    width_local = query_full.shape[1]
    inner_local = inner_full.shape[1]
    query_bias_here = lax.dynamic_slice_in_dim(
        query_bias_all, tensor_rank * width_local, width_local
    )
    value_bias_here = lax.dynamic_slice_in_dim(
        value_bias_all, tensor_rank * width_local, width_local
    )
    inner_bias_here = lax.dynamic_slice_in_dim(
        inner_bias_all, tensor_rank * inner_local, inner_local
    )
    seq_count = random_blocks.shape[0]
    seq_len = segment_ids.shape[0] // seq_count
    gather_ids, allowed = jax.vmap(block_layout)(
        segment_ids.reshape(seq_count, seq_len),
        pad_mask.reshape(seq_count, seq_len),
        random_blocks,
        global_blocks,
    )
    source_rows = lax.all_gather(layer_in, "tensor", axis=0, tiled=True)
    queries = (
        jnp.dot(source_rows, query_full, preferred_element_type=jnp.float32) + query_bias_here
    ).astype(jnp.bfloat16)
    keys_all = jnp.dot(source_rows, key_full, preferred_element_type=jnp.float32).astype(
        jnp.bfloat16
    )
    values_all = (
        jnp.dot(source_rows, value_full, preferred_element_type=jnp.float32) + value_bias_here
    ).astype(jnp.bfloat16)
    query_seq = queries.reshape(seq_count, seq_len, width_local)
    key_seq = keys_all.reshape(seq_count, seq_len, width_local)
    value_seq = values_all.reshape(seq_count, seq_len, width_local)
    attn_seq, log_totals = lax.map(
        attend_forward, (query_seq, key_seq, value_seq, gather_ids, allowed)
    )
    attn_flat = attn_seq.reshape(seq_count * seq_len, width_local)
    attn_proj = lax.psum_scatter(
        jnp.dot(attn_flat, output_full, preferred_element_type=jnp.float32).astype(jnp.bfloat16),
        "tensor",
        scatter_dimension=0,
        tiled=True,
    ).astype(jnp.float32)
    first_resid = layer_in.astype(jnp.float32) + attn_proj + output_bias_all
    first_norm, first_hat, first_inverse = layer_norm(first_resid, first_gain_all, first_shift_all)
    ffn_rows = lax.all_gather(first_norm.astype(jnp.bfloat16), "tensor", axis=0, tiled=True)
    inner_pre = jnp.dot(ffn_rows, inner_full, preferred_element_type=jnp.float32) + inner_bias_here
    inner_act, gelu_pull = jax.vjp(partial(jax.nn.gelu, approximate=False), inner_pre)
    hidden = inner_act.astype(jnp.bfloat16)
    ffn_out = lax.psum_scatter(
        jnp.dot(
            lax.slice_in_dim(hidden, 0, local_rows * lax.axis_size("tensor"), axis=0),
            outer_full,
            preferred_element_type=jnp.float32,
        ).astype(jnp.bfloat16),
        "tensor",
        scatter_dimension=0,
        tiled=True,
    ).astype(jnp.float32)
    second_resid = first_norm + ffn_out + outer_bias_all
    layer_out, second_hat, second_inverse = layer_norm(
        second_resid, second_gain_all, second_shift_all
    )
    grad_second_resid, grad_second_gain, grad_second_shift = norm_backward(
        output_grad.astype(jnp.float32), second_hat, second_inverse, second_gain_all
    )
    grad_outer_bias = jnp.sum(grad_second_resid, axis=0)
    grad_ffn_rows = lax.all_gather(
        grad_second_resid.astype(jnp.bfloat16), "tensor", axis=0, tiled=True
    )
    grad_outer_w = contract_rows(hidden, grad_ffn_rows)
    grad_hidden = contract_cols(grad_ffn_rows, outer_full)
    grad_inner = gelu_pull(grad_hidden)[0].astype(jnp.bfloat16)
    grad_inner_bias_here = jnp.sum(grad_inner.astype(jnp.float32), axis=0)
    grad_inner_w = contract_rows(ffn_rows, grad_inner)
    grad_first_norm = grad_second_resid + lax.psum_scatter(
        contract_cols(grad_inner, inner_full).astype(jnp.bfloat16),
        "tensor",
        scatter_dimension=0,
        tiled=True,
    ).astype(jnp.float32)
    grad_first_resid, grad_first_gain, grad_first_shift = norm_backward(
        grad_first_norm, first_hat, first_inverse, first_gain_all
    )
    grad_output_bias = jnp.sum(grad_first_resid, axis=0)
    grad_attn_rows = lax.all_gather(
        grad_first_resid.astype(jnp.bfloat16), "tensor", axis=0, tiled=True
    )
    grad_output_w = contract_rows(attn_flat, grad_attn_rows)
    grad_attn = contract_cols(grad_attn_rows, output_full).astype(jnp.bfloat16)
    grad_query_seq, grad_key_seq, grad_value_seq = lax.map(
        attend_backward,
        (
            query_seq,
            key_seq,
            value_seq,
            gather_ids,
            allowed,
            grad_attn.reshape(seq_count, seq_len, width_local),
            log_totals,
        ),
    )
    grad_queries = grad_query_seq.reshape(seq_count * seq_len, width_local).astype(jnp.bfloat16)
    grad_keys = grad_key_seq.reshape(seq_count * seq_len, width_local).astype(jnp.bfloat16)
    grad_values = grad_value_seq.reshape(seq_count * seq_len, width_local).astype(jnp.bfloat16)
    grad_query_bias_here = jnp.sum(grad_queries.astype(jnp.float32), axis=0)
    grad_value_bias_here = jnp.sum(grad_values.astype(jnp.float32), axis=0)
    grad_query_w = contract_rows(source_rows, grad_queries)
    grad_key_w = contract_rows(source_rows, grad_keys)
    grad_value_w = contract_rows(source_rows, grad_values)
    total = contract_cols(grad_queries, query_full)
    total = total + contract_cols(grad_keys, key_full)
    input_grad = grad_first_resid + lax.psum_scatter(
        (total + contract_cols(grad_values, value_full)).astype(jnp.bfloat16),
        "tensor",
        scatter_dimension=0,
        tiled=True,
    ).astype(jnp.float32)
    (
        query_grad_shard,
        key_grad_shard,
        value_grad_shard,
        output_grad_shard,
        inner_grad_shard,
        outer_grad_shard,
    ) = (
        lax.psum_scatter(grad_query_w, "dp", scatter_dimension=0, tiled=True),
        lax.psum_scatter(grad_key_w, "dp", scatter_dimension=0, tiled=True),
        lax.psum_scatter(grad_value_w, "dp", scatter_dimension=0, tiled=True),
        lax.psum_scatter(grad_output_w, "dp", scatter_dimension=1, tiled=True),
        lax.psum_scatter(grad_inner_w, "dp", scatter_dimension=0, tiled=True),
        lax.psum_scatter(grad_outer_w, "dp", scatter_dimension=1, tiled=True),
    )
    grad_query_bias = lax.dynamic_update_slice_in_dim(
        jnp.zeros_like(query_bias_all), grad_query_bias_here, tensor_rank * width_local, 0
    )
    grad_value_bias = lax.dynamic_update_slice_in_dim(
        jnp.zeros_like(value_bias_all), grad_value_bias_here, tensor_rank * width_local, 0
    )
    grad_inner_bias = lax.dynamic_update_slice_in_dim(
        jnp.zeros_like(inner_bias_all), grad_inner_bias_here, tensor_rank * inner_local, 0
    )
    (
        query_bias_shard,
        value_bias_shard,
        output_bias_shard,
        inner_bias_shard,
        outer_bias_shard,
        first_gain_shard,
        first_shift_shard,
        second_gain_shard,
        second_shift_shard,
    ) = (
        lax.psum_scatter(grad_query_bias, ("dp", "tensor"), scatter_dimension=0, tiled=True),
        lax.psum_scatter(grad_value_bias, ("dp", "tensor"), scatter_dimension=0, tiled=True),
        lax.psum_scatter(grad_output_bias, ("dp", "tensor"), scatter_dimension=0, tiled=True),
        lax.psum_scatter(grad_inner_bias, ("dp", "tensor"), scatter_dimension=0, tiled=True),
        lax.psum_scatter(grad_outer_bias, ("dp", "tensor"), scatter_dimension=0, tiled=True),
        lax.psum_scatter(grad_first_gain, ("dp", "tensor"), scatter_dimension=0, tiled=True),
        lax.psum_scatter(grad_first_shift, ("dp", "tensor"), scatter_dimension=0, tiled=True),
        lax.psum_scatter(grad_second_gain, ("dp", "tensor"), scatter_dimension=0, tiled=True),
        lax.psum_scatter(grad_second_shift, ("dp", "tensor"), scatter_dimension=0, tiled=True),
    )
    return (
        layer_out.astype(jnp.bfloat16),
        input_grad,
        query_grad_shard,
        key_grad_shard,
        value_grad_shard,
        output_grad_shard,
        inner_grad_shard,
        outer_grad_shard,
        query_bias_shard,
        value_bias_shard,
        output_bias_shard,
        inner_bias_shard,
        outer_bias_shard,
        first_gain_shard,
        first_shift_shard,
        second_gain_shard,
        second_shift_shard,
    )


def solution(mesh):
    return jax.shard_map(
        on_device,
        mesh=mesh,
        in_specs=(
            P(("dp", "tensor"), None),
            P("dp", "tensor"),
            P("dp", "tensor"),
            P("dp", "tensor"),
            P("tensor", "dp"),
            P("dp", "tensor"),
            P("tensor", "dp"),
            P(("dp", "tensor")),
            P(("dp", "tensor")),
            P(("dp", "tensor")),
            P(("dp", "tensor")),
            P(("dp", "tensor")),
            P(("dp", "tensor")),
            P(("dp", "tensor")),
            P(("dp", "tensor")),
            P(("dp", "tensor")),
            P("dp"),
            P("dp"),
            P("dp", None, None),
            P("dp", None, None),
            P(("dp", "tensor"), None),
        ),
        out_specs=(
            P(("dp", "tensor"), None),
            P(("dp", "tensor"), None),
            P("dp", "tensor"),
            P("dp", "tensor"),
            P("dp", "tensor"),
            P("tensor", "dp"),
            P("dp", "tensor"),
            P("tensor", "dp"),
            P(("dp", "tensor")),
            P(("dp", "tensor")),
            P(("dp", "tensor")),
            P(("dp", "tensor")),
            P(("dp", "tensor")),
            P(("dp", "tensor")),
            P(("dp", "tensor")),
            P(("dp", "tensor")),
            P(("dp", "tensor")),
        ),
        check_vma=False,
    )
```

profile of v0, /device:TPU:0, one launch (start us, length us, event | category | flops | bytes accessed | tf_op | source)
XLA Modules:
  0.0 2189.0 jit_solution(9100617027004236534)
XLA Ops:
  16.2 43.7 %all-reduce.19 = (f32[768]{0:T(1024)}, f32[768]{0:T(1024)}, f32[768]{0:T(1024)S(1)}, f32[768]{0:T(1024)S(1)}, f32[768]{0:T(1024)}, /*index=5*/f32[3072]{0:T(1024)}, f32[768]{0:T(1024)}, f32[768]{0:T(1024)}) all-reduce(f32[768]{0:T(1024)S(1)} %dynamic-update-slice.4, ...), channel_id=1, replica_groups=mesh['dp'=8,'tensor'=4] {'dp','tensor'}, use_global_device_ids=true, to_apply=%add.4 | all-reduce | flops 8448 | bytes 67584
  77.2 33.0 %all_gather.63 = bf16[192,768]{0,1:T(8,128)(2,1)} all-gather(bf16[192,96]{0,1:T(8,128)(2,1)S(1)} %copy.246), channel_id=1, replica_groups=mesh['dp'=8,'tensor'=4] {'dp'}, dimensions={1}, use_global_device_ids=true | all-gather | bytes 331776 | tf_op jit(solution)/shard_map/all_gather | solution.py:191
  110.2 31.2 %all_gather.60 = bf16[768,192]{1,0:T(8,128)(2,1)S(1)} all-gather(bf16[96,192]{1,0:T(8,128)(2,1)S(1)} %copy-done.36), channel_id=1, replica_groups=mesh['dp'=8,'tensor'=4] {'dp'}, dimensions={0}, use_global_device_ids=true | all-gather | bytes 331776 | tf_op jit(solution)/shard_map/all_gather | solution.py:187
  141.4 31.0 %all_gather.62 = bf16[768,192]{1,0:T(8,128)(2,1)S(1)} all-gather(bf16[96,192]{1,0:T(8,128)(2,1)S(1)} %copy-done.37), channel_id=1, replica_groups=mesh['dp'=8,'tensor'=4] {'dp'}, dimensions={0}, use_global_device_ids=true | all-gather | bytes 331776 | tf_op jit(solution)/shard_map/all_gather | solution.py:188
  172.3 31.3 %all_gather.58 = bf16[768,192]{1,0:T(8,128)(2,1)S(1)} all-gather(bf16[96,192]{1,0:T(8,128)(2,1)S(1)} %copy-done.38), channel_id=1, replica_groups=mesh['dp'=8,'tensor'=4] {'dp'}, dimensions={0}, use_global_device_ids=true | all-gather | bytes 331776 | tf_op jit(solution)/shard_map/all_gather | solution.py:189
  204.0 15.2 and_and_fusion
  232.2 250.3 %while.26 = (s32[]{:T(128)}, bf16[2,2048,192]{1,2,0:T(8,128)(2,1)}, f32[2,32,3,64,1,1]{3,2,1,5,4,0:T(4,128)}, bf16[2,2048,192]{1,2,0:T(8,128)(2,1)}, s32[2,32,10...) while((s32[]{:T(128)}, bf16[2,2048,192]{1,2,0:T(8,128)(2,1)}, ...), condition=%wide.region_6.7_spmd, body=%wide.region_3.6_spmd.sunk | while | flops 1054207936 | bytes 222811088 | solution.py:247
  253.0 12.7 gather_fusion
  265.7 13.6 copy.338
  279.3 12.6 gather_fusion.1
  291.9 15.9 fusion.131
  307.7 13.9 fusion.132
  334.8 18.8 fusion.134
  377.9 12.7 gather_fusion
  390.6 13.6 copy.338
  404.1 12.6 gather_fusion.1
  416.7 15.9 fusion.131
  432.6 13.9 fusion.132
  459.6 18.8 fusion.134
  490.4 57.9 %reduce-scatter.19.cloned.1.call-done = bf16[1024,768]{1,0:T(8,128)(2,1)} async-done(((bf16[4096,768]{1,0:T(8,128)(2,1)}), bf16[1024,768]{1,0:T(8,128)(2,1)}) %reduce-scatter.19.cloned.1.call-update) | async-done | bytes 1572880 | tf_op jit(solution)/shard_map/reduce_scatter | solution.py:251
  556.3 44.9 %all-gather.9.cloned.1.call-done = bf16[4096,768]{1,0:T(8,128)(2,1)} async-done(((bf16[1024,768]{1,0:T(8,128)(2,1)}), bf16[4096,768]{1,0:T(8,128)(2,1)}) %all-gather.9.cloned.1.call-update) | async-done | bytes 6291472 | tf_op jit(solution)/shard_map/all_gather | solution.py:259
  601.2 34.8 %multiply_convert_fusion.1 = (bf16[4096,768]{1,0:T(8,128)(2,1)}, f32[4096,768]{1,0:T(8,128)}, f32[4096,768]{1,0:T(8,128)}) fusion(f32[768]{0:T(1024)S(1)} %dynamic_slice.51, bf16[4096,768]{1,0:T(8,128)(2,1)} %all-gather.9.cloned.1.call-done, bf16[768,768]{1,0:T(8,128)(2,1)} %all-gather.11.cloned.1.call-done), kind=kOutput, calls=%fused_computation.69 | convolution fusion | flops 5039456256 | bytes 38931456 | tf_op jit(solution)/shard_map/dot_general | solution.py:260
  654.4 56.8 %reduce-scatter.21.cloned.1.call-done = bf16[1024,768]{1,0:T(8,128)(2,1)} async-done(((bf16[4096,768]{1,0:T(8,128)(2,1)}), bf16[1024,768]{1,0:T(8,128)(2,1)}) %reduce-scatter.21.cloned.1.call-update) | async-done | bytes 1572880 | tf_op jit(solution)/shard_map/reduce_scatter | solution.py:263
  720.2 46.5 %all-gather.15.cloned.1.call-done = bf16[4096,768]{1,0:T(8,128)(2,1)} async-done(((bf16[1024,768]{1,0:T(8,128)(2,1)}), bf16[4096,768]{1,0:T(8,128)(2,1)}) %all-gather.15.cloned.1.call-update) | async-done | bytes 6291472 | tf_op jit(solution)/shard_map/all_gather | solution.py:281
  766.7 19.2 convert_reduce_fusion
  795.6 58.3 %reduce-scatter.23.cloned.1.call-done = bf16[1024,768]{1,0:T(8,128)(2,1)} async-done(((bf16[4096,768]{1,0:T(8,128)(2,1)}), bf16[1024,768]{1,0:T(8,128)(2,1)}) %reduce-scatter.23.cloned.1.call-update) | async-done | bytes 1572880 | tf_op jit(solution)/shard_map/reduce_scatter | solution.py:289
  863.9 46.5 %all-gather.17.cloned.1.call-done = bf16[4096,768]{1,0:T(8,128)(2,1)} async-done(((bf16[1024,768]{1,0:T(8,128)(2,1)}), bf16[4096,768]{1,0:T(8,128)(2,1)}) %all-gather.17.cloned.1.call-update) | async-done | bytes 6291472 | tf_op jit(solution)/shard_map/all_gather | solution.py:299
  916.6 790.0 %while.27 = (s32[]{:T(128)}, bf16[2,2048,192]{1,2,0:T(8,128)(2,1)}, bf16[2,2048,192]{1,2,0:T(8,128)(2,1)}, bf16[2,2048,192]{1,2,0:T(8,128)(2,1)}, bf16[2,2048,19...) while((s32[]{:T(128)}, bf16[2,2048,192]{1,2,0:T(8,128)(2,1)}, ...), condition=%wide.region_22.23_spmd, body=%wide.region_18.22_spmd.sunk | while | flops 2588143616 | bytes 472057440 | solution.py:304
  941.7 12.7 gather_fusion.3
  954.4 12.7 gather_fusion.2
  967.1 13.6 copy.347
  980.8 15.8 fusion.145
  996.6 13.6 copy.349
  1010.2 15.9 fusion.146
  1026.1 20.7 multiply_reduce_fusion.9
  1046.8 26.0 %multiply_convert_fusion.3 = bf16[32,3,64,10,64]{2,4,3,1,0:T(8,128)(2,1)} fusion(f32[32,3,64,10,64]{2,4,3,1,0:T(8,128)} %bitcast.241, f32[32,3,64,10,64]{2,4,3,1,0:T(8,128)} %bitcast.235, f32[32,3,64]{2,1,0:T(4,128)S(1)} %multiply_reduce_fusion.9, f32[32,3,64]{2,1,0:T(4,128)S(1)} %dynamic-slice_bitcast_fusion.7, pred[32,64,10,64]{1,3,2,0:T(8,128)(4,1)S(1)} %copy-done.1), kind=kLoop, calls=%fused_computation.31.clone.1 | loop fusion | flops 23592960 | bytes 40681472 | tf_op jit(solution)/shard_map/while/body/eval_jaxpr/convert_element_type | solution.py:112
  1072.8 13.5 fusion.147
  1086.2 29.4 %fusion.148 = f32[32,10,64,3,64]{2,4,1,3,0:T(8,128)} fusion(f32[32,3,64,10,64]{2,4,3,1,0:T(8,128)} %bitcast.236, f32[32,3,64]{2,1,0:T(4,128)S(1)} %dynamic-slice_bitcast_fusion.7, pred[32,64,10,64]{1,3,2,0:T(8,128)(4,1)S(1)} %copy-done.1, bf16[32,64,3,64,1]{1,0,3,2,4:T(8,128)(2,1)S(1)} %bitcast.253), kind=kOutput, calls=%fused_computation.40.clone.1 | convolution fusion | flops 519045120 | bytes 33579008 | tf_op jit(solution)/shard_map/while/body/eval_jaxpr/ihaec,iahd->iechd/dot_general | solution.py:119
  1115.7 30.8 %copy.353 = f32[32,10,64,3,64]{4,2,3,1,0:T(8,128)} copy(f32[32,10,64,3,64]{2,4,1,3,0:T(8,128)} %fusion.148) | data formatting | bytes 31457280 | tf_op jit(solution)/shard_map/while/body/eval_jaxpr/ihaec,iahd->iechd/transpose | solution.py:119
  1146.9 51.0 %scatter_fusion.1 = f32[32,64,3,64]{3,1,2,0:T(8,128)S(1)} fusion(f32[32,64,3,64]{3,1,2,0:T(8,128)S(1)} %broadcast.435.clone.1, s32[320]{0:T(512)S(1)} %copy-done.16, f32[320,64,3,64]{3,1,2,0:T(8,128)} %bitcast.243), kind=kCustom, calls=%fused_computation.7.clone.1 | custom fusion | flops 3932160 | bytes 47187200 | tf_op jit(solution)/shard_map/while/body/eval_jaxpr/scatter-add | solution.py:124
  1210.6 15.7 multiply_bitcast_fusion.2
  1226.3 22.7 %copy.350 = f32[32,10,64,3,64]{4,2,3,1,0:T(8,128)} copy(f32[32,10,64,3,64]{4,2,1,3,0:T(8,128)} %multiply_bitcast_fusion.2) | data formatting | bytes 31457280 | tf_op jit(solution)/shard_map/while/body/eval_jaxpr/mul | solution.py:116
  1249.5 51.0 %scatter_fusion = f32[32,64,3,64]{3,1,2,0:T(8,128)S(1)} fusion(f32[32,64,3,64]{3,1,2,0:T(8,128)S(1)} %broadcast.435.clone, s32[320]{0:T(512)S(1)} %copy-done.16, f32[320,64,3,64]{3,1,2,0:T(8,128)} %bitcast.242), kind=kCustom, calls=%fused_computation.6.clone.1 | custom fusion | flops 3932160 | bytes 47187200 | tf_op jit(solution)/shard_map/while/body/eval_jaxpr/scatter-add | solution.py:123
  1333.0 12.7 gather_fusion.3
  1345.7 12.7 gather_fusion.2
  1358.4 13.6 copy.347
  1372.0 15.8 fusion.145
  1387.8 13.6 copy.349
  1401.5 15.9 fusion.146
  1417.4 20.7 multiply_reduce_fusion.9
  1438.1 26.0 %multiply_convert_fusion.3 = bf16[32,3,64,10,64]{2,4,3,1,0:T(8,128)(2,1)} fusion(f32[32,3,64,10,64]{2,4,3,1,0:T(8,128)} %bitcast.241, f32[32,3,64,10,64]{2,4,3,1,0:T(8,128)} %bitcast.235, f32[32,3,64]{2,1,0:T(4,128)S(1)} %multiply_reduce_fusion.9, f32[32,3,64]{2,1,0:T(4,128)S(1)} %dynamic-slice_bitcast_fusion.7, pred[32,64,10,64]{1,3,2,0:T(8,128)(4,1)S(1)} %copy-done.1), kind=kLoop, calls=%fused_computation.31.clone.1 | loop fusion | flops 23592960 | bytes 40681472 | tf_op jit(solution)/shard_map/while/body/eval_jaxpr/convert_element_type | solution.py:112
  1464.0 13.5 fusion.147
  1477.5 29.6 %fusion.148 = f32[32,10,64,3,64]{2,4,1,3,0:T(8,128)} fusion(f32[32,3,64,10,64]{2,4,3,1,0:T(8,128)} %bitcast.236, f32[32,3,64]{2,1,0:T(4,128)S(1)} %dynamic-slice_bitcast_fusion.7, pred[32,64,10,64]{1,3,2,0:T(8,128)(4,1)S(1)} %copy-done.1, bf16[32,64,3,64,1]{1,0,3,2,4:T(8,128)(2,1)S(1)} %bitcast.253), kind=kOutput, calls=%fused_computation.40.clone.1 | convolution fusion | flops 519045120 | bytes 33579008 | tf_op jit(solution)/shard_map/while/body/eval_jaxpr/ihaec,iahd->iechd/dot_general | solution.py:119
  1507.1 30.8 %copy.353 = f32[32,10,64,3,64]{4,2,3,1,0:T(8,128)} copy(f32[32,10,64,3,64]{2,4,1,3,0:T(8,128)} %fusion.148) | data formatting | bytes 31457280 | tf_op jit(solution)/shard_map/while/body/eval_jaxpr/ihaec,iahd->iechd/transpose | solution.py:119
  1538.3 51.0 %scatter_fusion.1 = f32[32,64,3,64]{3,1,2,0:T(8,128)S(1)} fusion(f32[32,64,3,64]{3,1,2,0:T(8,128)S(1)} %broadcast.435.clone.1, s32[320]{0:T(512)S(1)} %copy-done.16, f32[320,64,3,64]{3,1,2,0:T(8,128)} %bitcast.243), kind=kCustom, calls=%fused_computation.7.clone.1 | custom fusion | flops 3932160 | bytes 47187200 | tf_op jit(solution)/shard_map/while/body/eval_jaxpr/scatter-add | solution.py:124
  1602.1 15.7 multiply_bitcast_fusion.2
  1617.8 22.5 %copy.350 = f32[32,10,64,3,64]{4,2,3,1,0:T(8,128)} copy(f32[32,10,64,3,64]{4,2,1,3,0:T(8,128)} %multiply_bitcast_fusion.2) | data formatting | bytes 31457280 | tf_op jit(solution)/shard_map/while/body/eval_jaxpr/mul | solution.py:116
  1640.7 51.0 %scatter_fusion = f32[32,64,3,64]{3,1,2,0:T(8,128)S(1)} fusion(f32[32,64,3,64]{3,1,2,0:T(8,128)S(1)} %broadcast.435.clone, s32[320]{0:T(512)S(1)} %copy-done.16, f32[320,64,3,64]{3,1,2,0:T(8,128)} %bitcast.242), kind=kCustom, calls=%fused_computation.6.clone.1 | custom fusion | flops 3932160 | bytes 47187200 | tf_op jit(solution)/shard_map/while/body/eval_jaxpr/scatter-add | solution.py:123
  1791.6 40.8 %all-reduce.18 = (f32[768]{0:T(1024)S(1)}, f32[768]{0:T(1024)S(1)}, f32[768]{0:T(1024)S(1)}, f32[768]{0:T(1024)S(1)}, f32[3072]{0:T(1024)S(1)}, /*index=5*/f32[7...) all-reduce(f32[768]{0:T(1024)S(1)} %dynamic-update-slice.8, ...), channel_id=1, replica_groups=mesh['dp'=8,'tensor'=4] {'dp','tensor'}, use_global_device_ids=true, to_apply=%add.8 | all-reduce | flops 9984 | bytes 79872
  1845.3 66.4 %reduce-scatter.27.cloned.1.call-done = f32[96,768]{1,0:T(8,128)} async-done(((f32[768,768]{1,0:T(8,128)}), f32[96,768]{1,0:T(8,128)}) %reduce-scatter.27.cloned.1.call-update) | async-done | bytes 294928 | tf_op jit(solution)/shard_map/reduce_scatter | solution.py:344
  1911.7 72.6 %reduce-scatter.29.cloned.1.call-done = f32[768,96]{0,1:T(8,128)} async-done(((f32[768,768]{0,1:T(8,128)}), f32[768,96]{0,1:T(8,128)}) %reduce-scatter.29.cloned.1.call-update) | async-done | bytes 294928 | tf_op jit(solution)/shard_map/reduce_scatter | solution.py:345
  1984.3 65.9 %reduce-scatter.33.cloned.1.call-done = f32[96,192]{1,0:T(8,128)} async-done(((f32[768,192]{1,0:T(8,128)}), f32[96,192]{1,0:T(8,128)}) %reduce-scatter.33.cloned.1.call-update) | async-done | bytes 73744
  2050.1 65.4 %reduce-scatter.31.cloned.1.call-done = f32[96,192]{1,0:T(8,128)} async-done(((f32[768,192]{1,0:T(8,128)}), f32[96,192]{1,0:T(8,128)}) %reduce-scatter.31.cloned.1.call-update) | async-done | bytes 73744
  2115.5 65.8 %reduce-scatter.35.cloned.1.call-done = f32[96,192]{1,0:T(8,128)} async-done(((f32[768,192]{1,0:T(8,128)}), f32[96,192]{1,0:T(8,128)}) %reduce-scatter.35.cloned.1.call-update) | async-done | bytes 73744
  (371 shorter events, 371.4 us)
Async XLA Ops:
  8.0 211.2 %all-gather.7.cloned.1.call-start = ((), (), s32[]{:S(2)}) async-start(), calls=%async_computation.10 | async-start | bytes 7864320 | tf_op jit(solution)/shard_map/all_gather | solution.py:234
  8.8 539.6 %reduce-scatter.19.cloned.1.call-start = ((), (), s32[]{:S(2)}) async-start(), calls=%async_computation.11 | async-start | bytes 7864320 | tf_op jit(solution)/shard_map/reduce_scatter | solution.py:251
  66.3 43.9 %copy-start.36 = (bf16[96,192]{1,0:T(8,128)(2,1)S(1)}, bf16[96,192]{1,0:T(8,128)(2,1)}, u32[]{:S(2)}) copy-start(bf16[96,192]{1,0:T(8,128)(2,1)} %param.30) | copy-start | bytes 110596
  66.3 75.1 %copy-start.37 = (bf16[96,192]{1,0:T(8,128)(2,1)S(1)}, bf16[96,192]{1,0:T(8,128)(2,1)}, u32[]{:S(2)}) copy-start(bf16[96,192]{1,0:T(8,128)(2,1)} %param.31) | copy-start | bytes 110596
  71.5 100.8 %copy-start.38 = (bf16[96,192]{1,0:T(8,128)(2,1)S(1)}, bf16[96,192]{1,0:T(8,128)(2,1)}, u32[]{:S(2)}) copy-start(bf16[96,192]{1,0:T(8,128)(2,1)} %param.32) | copy-start | bytes 110596
  71.5 132.2 %copy-start.50 = (pred[10]{0:T(512)(128)(4,1)S(1)}, pred[10]{0:T(512)(128)(4,1)}, u32[]{:S(2)}) copy-start(pred[10]{0:T(512)(128)(4,1)} %constant.186) | copy-start | bytes 34
  71.5 132.2 %copy-start.51 = (pred[10]{0:T(512)(128)(4,1)S(1)}, pred[10]{0:T(512)(128)(4,1)}, u32[]{:S(2)}) copy-start(pred[10]{0:T(512)(128)(4,1)} %constant.185) | copy-start | bytes 34
  71.5 132.2 %copy-start.52 = (pred[10]{0:T(512)(128)(4,1)S(1)}, pred[10]{0:T(512)(128)(4,1)}, u32[]{:S(2)}) copy-start(pred[10]{0:T(512)(128)(4,1)} %constant.184) | copy-start | bytes 34
  141.4 86.6 %copy-start.28 = (bf16[768,192]{1,0:T(8,128)(2,1)}, bf16[768,192]{1,0:T(8,128)(2,1)S(1)}, u32[]{:S(2)}) copy-start(bf16[768,192]{1,0:T(8,128)(2,1)S(1)} %all_gather.60) | copy-start | bytes 884740
  172.3 53.3 %copy-start.24 = (bf16[768,192]{1,0:T(8,128)(2,1)}, bf16[768,192]{1,0:T(8,128)(2,1)S(1)}, u32[]{:S(2)}) copy-start(bf16[768,192]{1,0:T(8,128)(2,1)S(1)} %all_gather.62) | copy-start | bytes 884740
  203.7 20.7 copy-start.26
  232.2 253.1 %copy-start.22 = (bf16[192,768]{0,1:T(8,128)(2,1)S(1)}, bf16[192,768]{0,1:T(8,128)(2,1)}, u32[]{:S(2)}) copy-start(bf16[192,768]{0,1:T(8,128)(2,1)} %all_gather.63) | copy-start | bytes 884740
  279.3 12.6 copy-start.7
  291.9 15.9 copy-start.2
  307.7 19.0 copy-start
  404.1 12.6 copy-start.7
  416.7 15.9 copy-start.2
  432.6 19.0 copy-start
  489.8 58.6 %copy-start.10 = (bf16[1024,768]{1,0:T(8,128)(2,1)S(1)}, bf16[1024,768]{1,0:T(8,128)(2,1)}, u32[]{:S(2)}) copy-start(bf16[1024,768]{1,0:T(8,128)(2,1)} %param.29) | copy-start | bytes 4718596
  489.8 58.6 %copy-start.30 = (f32[768]{0:T(1024)S(1)}, f32[768]{0:T(1024)}, u32[]{:S(2)}) copy-start(f32[768]{0:T(1024)} %get-tuple-element.369) | copy-start | bytes 9220
  489.8 63.0 %copy-start.33 = (f32[768]{0:T(1024)S(1)}, f32[768]{0:T(1024)}, u32[]{:S(2)}) copy-start(f32[768]{0:T(1024)} %get-tuple-element.366) | copy-start | bytes 9220
  489.8 63.0 %copy-start.45 = (f32[768]{0:T(1024)S(1)}, f32[768]{0:T(1024)}, u32[]{:S(2)}) copy-start(f32[768]{0:T(1024)} %get-tuple-element.365) | copy-start | bytes 9220
  489.8 66.5 %all-gather.11.cloned.1.call-start = ((), (), s32[]{:S(2)}) async-start(), calls=%async_computation.13 | async-start | bytes 1327104 | tf_op jit(solution)/shard_map/all_gather | solution.py:190
  490.4 110.8 %all-gather.9.cloned.1.call-start = ((), (), s32[]{:S(2)}) async-start(), calls=%async_computation.12 | async-start | bytes 7864320 | tf_op jit(solution)/shard_map/all_gather | solution.py:259
  554.8 90.2 %all-gather.13.cloned.1.call-start = ((), (), s32[]{:S(2)}) async-start(), calls=%async_computation.14 | async-start | bytes 1327104 | tf_op jit(solution)/shard_map/all_gather | solution.py:192
  555.4 155.7 %reduce-scatter.21.cloned.1.call-start = ((), (), s32[]{:S(2)}) async-start(), calls=%async_computation.15 | async-start | bytes 7864320 | tf_op jit(solution)/shard_map/reduce_scatter | solution.py:263
  654.3 56.9 %copy-start.48 = (f32[768]{0:T(1024)S(1)}, f32[768]{0:T(1024)}, u32[]{:S(2)}) copy-start(f32[768]{0:T(1024)} %get-tuple-element.371) | copy-start | bytes 9220
  654.3 112.3 %all-gather.15.cloned.1.call-start = ((), (), s32[]{:S(2)}) async-start(), calls=%async_computation.16 | async-start | bytes 7864320 | tf_op jit(solution)/shard_map/all_gather | solution.py:281
  720.1 133.8 %reduce-scatter.23.cloned.1.call-start = ((), (), s32[]{:S(2)}) async-start(), calls=%async_computation.17 | async-start | bytes 7864320 | tf_op jit(solution)/shard_map/reduce_scatter | solution.py:289
  766.7 19.2 copy-start.53
  795.6 114.8 %all-gather.17.cloned.1.call-start = ((), (), s32[]{:S(2)}) async-start(), calls=%async_computation.18 | async-start | bytes 7864320 | tf_op jit(solution)/shard_map/all_gather | solution.py:299
  860.8 49.5 %copy-start.23 = (bf16[192,768]{0,1:T(8,128)(2,1)S(1)}, bf16[192,768]{0,1:T(8,128)(2,1)}, u32[]{:S(2)}) copy-start(bf16[192,768]{0,1:T(8,128)(2,1)} %all_gather.63) | copy-start | bytes 884740
  863.8 975.5 %reduce-scatter.37.cloned.1.call-start = ((), (), s32[]{:S(2)}) async-start(), calls=%async_computation.25 | async-start | bytes 884736
  967.1 13.6 copy-start.5
  996.6 13.6 copy-start.3
  1010.2 15.9 copy-start.1
  1072.8 13.5 copy-start.6
  1115.7 31.2 %copy-start.16 = (s32[320]{0:T(512)S(1)}, s32[320]{0:T(512)}, u32[]{:S(2)}) copy-start(s32[320]{0:T(512)} %copy-done.15) | copy-start | bytes 3844 | tf_op jit(solution)/shard_map/while
  1200.4 10.3 copy-start.4
  1358.4 13.6 copy-start.5
  1387.8 13.6 copy-start.3
  1401.5 15.9 copy-start.1
  1464.0 13.5 copy-start.6
  1507.1 31.2 %copy-start.16 = (s32[320]{0:T(512)S(1)}, s32[320]{0:T(512)}, u32[]{:S(2)}) copy-start(s32[320]{0:T(512)} %copy-done.15) | copy-start | bytes 3844 | tf_op jit(solution)/shard_map/while
  1591.8 10.3 copy-start.4
  1714.9 126.1 %reduce-scatter.25.cloned.1.call-start = ((), (), s32[]{:S(2)}) async-start(), calls=%async_computation.19 | async-start | bytes 7864320 | tf_op jit(solution)/shard_map/reduce_scatter | solution.py:326
  1718.1 12.8 copy-start.18
  1743.3 168.4 %reduce-scatter.27.cloned.1.call-start = ((), (), s32[]{:S(2)}) async-start(), calls=%async_computation.20 | async-start | bytes 2654208 | tf_op jit(solution)/shard_map/reduce_scatter | solution.py:344
  1753.5 230.8 %reduce-scatter.29.cloned.1.call-start = ((), (), s32[]{:S(2)}) async-start(), calls=%async_computation.21 | async-start | bytes 2654208 | tf_op jit(solution)/shard_map/reduce_scatter | solution.py:345
  1763.9 286.2 %reduce-scatter.33.cloned.1.call-start = ((), (), s32[]{:S(2)}) async-start(), calls=%async_computation.23 | async-start | bytes 884736
  1771.4 344.1 %reduce-scatter.31.cloned.1.call-start = ((), (), s32[]{:S(2)}) async-start(), calls=%async_computation.22 | async-start | bytes 884736
  1778.8 7.8 copy-start.54
  1778.8 8.0 copy-start.49
  1778.8 402.5 %reduce-scatter.35.cloned.1.call-start = ((), (), s32[]{:S(2)}) async-start(), calls=%async_computation.24 | async-start | bytes 884736
  1783.9 7.7 copy-start.41
  1783.9 7.7 copy-start.42
  1783.9 7.7 copy-start.43
  1783.9 7.7 copy-start.44
  1783.9 7.7 copy-start.46
  1783.9 7.7 copy-start.47
  1783.9 53.7 %copy-start.9 = (f32[1024,768]{1,0:T(8,128)S(1)}, f32[1024,768]{1,0:T(8,128)}, u32[]{:S(2)}) copy-start(f32[1024,768]{1,0:T(8,128)} %copy-done.8) | copy-start | bytes 9437188
  1783.9 53.7 %copy-start.32 = (f32[1024]{0:T(1024)S(1)}, f32[1024]{0:T(1024)}, u32[]{:S(2)}) copy-start(f32[1024]{0:T(1024)} %copy-done.31) | copy-start | bytes 12292
  1783.9 53.7 %copy-start.35 = (f32[1024]{0:T(1024)S(1)}, f32[1024]{0:T(1024)}, u32[]{:S(2)}) copy-start(f32[1024]{0:T(1024)} %copy-done.34) | copy-start | bytes 12292
  1783.9 53.7 %copy-start.40 = (f32[768]{0:T(1024)S(1)}, f32[768]{0:T(1024)}, u32[]{:S(2)}) copy-start(f32[768]{0:T(1024)} %get-tuple-element.372) | copy-start | bytes 9220
  (17 other events, 71.7 us)
Sparse Core Ops, SparseCore 0:
  10.4 50.5 all-gather.6
  489.9 58.4 reduce-scatter.18
  720.2 46.3 all-gather.14
  864.0 46.3 all-gather.16
Sparse Core Ops, SparseCore 1:
  492.5 41.5 all-gather.10
  554.9 46.2 all-gather.8
  603.5 41.5 all-gather.12
  654.4 56.7 reduce-scatter.20
  795.6 58.2 reduce-scatter.22
  1715.0 62.6 reduce-scatter.36
  1780.0 58.2 reduce-scatter.24
  1842.5 69.1 reduce-scatter.26
  1916.0 68.2 reduce-scatter.28
  1988.5 61.6 reduce-scatter.32
  2053.9 61.6 reduce-scatter.30
  2119.8 61.5 reduce-scatter.34
where the time goes:
time: 2200 us; the launch traced here: 2190 us
  waiting for transfers between devices  658 us (30%)
  local copies, waits for them, and re-layouts  487 us (22%)
  matrix products  410 us (19%)
  other arithmetic  397 us (18%)
  blocking collectives  211 us (10%)
    unnamed x20, waiting for transfers between devices  199 us
    gather x8, local copies, waits for them, and re-layouts, block_operands(): key_blocks = keys.reshape(key_count, block_size, heads_here, HD)[gather_ids]  105 us
    scatter-add x2, other arithmetic, attend_backward(): grad_key = empty.at[gather_ids].add(key_parts)  102 us
    scatter-add x2, other arithmetic, attend_backward(): grad_value = empty.at[gather_ids].add(value_parts)  102 us
    while x6, matrix products  95.2 us
    unnamed x2, blocking collectives  84.5 us
    gather x6, local copies, waits for them, and re-layouts, block_operands(): values.reshape(key_count, block_size, heads_here, HD)[gather_ids]  77.8 us
    reduce_scatter x1, waiting for transfers between devices, on_device(): lax.psum_scatter(grad_outer_w, 'dp', scatter_dimension=1, tiled=True)  72.6 us
  transfers between devices with their start and end apart: 16, of which 12 were waited for; matrix products, arithmetic and copies ran while one was open for 8% of the time, Pallas kernels for 0%

commit v1 on v0

v1 whole, which is shorter than its diff:
```python
from functools import partial

import jax
import jax.numpy as jnp
from jax import lax
from jax.experimental import pallas as pl
from jax.experimental.pallas import tpu as pltpu
from jax.sharding import PartitionSpec as P

HD = 64
PAIR = 2 * HD
QT = 256
KT = 128
EPSILON = 1e-06
NEGATIVE = -1e30
MESH = pl.DeviceIdType.MESH
VMEM_LIMIT = 56 * 2**20
BF = jnp.bfloat16
F32 = jnp.float32


def params_of(collective_id=None):
    if collective_id is None:
        return pltpu.CompilerParams(vmem_limit_bytes=VMEM_LIMIT)
    return pltpu.CompilerParams(
        vmem_limit_bytes=VMEM_LIMIT, collective_id=collective_id, has_side_effects=True
    )


def nt(left, right, **more):
    return lax.dot_general(
        left, right, (((1,), (1,)), ((), ())), preferred_element_type=F32, **more
    )


def nn(left, right):
    return lax.dot_general(left, right, (((1,), (0,)), ((), ())), preferred_element_type=F32)


def tn(left, right):
    return lax.dot_general(left, right, (((0,), (0,)), ((), ())), preferred_element_type=F32)


def sibling_of():
    rank = lax.axis_index("tensor")
    half = lax.rem(rank, 2)
    return half, {"tensor": rank + 1 - 2 * half}


def meet(sibling):
    barrier = pltpu.get_barrier_semaphore()
    pl.semaphore_signal(barrier, inc=1, device_id=sibling, device_id_type=MESH)
    pl.semaphore_wait(barrier, 1)


def gather_pair_kernel(first, qkv_ref, both_ref, local_sem, send_sem, recv_sem):
    half, sibling = sibling_of()
    meet(sibling)
    own = qkv_ref.at[:, first:]
    away = pltpu.make_async_remote_copy(
        own, both_ref.at[half], send_sem, recv_sem, device_id=sibling, device_id_type=MESH
    )
    away.start()
    here = pltpu.make_async_copy(own, both_ref.at[half], local_sem)
    here.start()
    here.wait()
    away.wait()


def gather_pair(qkv, first):
    rows, width = qkv.shape[0], qkv.shape[1] - first
    return pl.pallas_call(
        partial(gather_pair_kernel, first),
        name="gather_pair",
        out_shape=jax.ShapeDtypeStruct((2, rows, width), qkv.dtype),
        in_specs=[pl.BlockSpec(memory_space=pl.ANY)],
        out_specs=pl.BlockSpec(memory_space=pl.ANY),
        scratch_shapes=[pltpu.SemaphoreType.DMA(())] * 3,
        compiler_params=params_of(1),
    )(qkv)


def swap_pair_kernel(both_ref, other_ref, send_sem, recv_sem):
    half, sibling = sibling_of()
    meet(sibling)
    away = pltpu.make_async_remote_copy(
        both_ref.at[1 - half], other_ref, send_sem, recv_sem,
        device_id=sibling, device_id_type=MESH,
    )
    away.start()
    away.wait()


def swap_pair(both):
    return pl.pallas_call(
        swap_pair_kernel,
        name="swap_pair",
        out_shape=jax.ShapeDtypeStruct(both.shape[1:], both.dtype),
        in_specs=[pl.BlockSpec(memory_space=pl.ANY)],
        out_specs=pl.BlockSpec(memory_space=pl.ANY),
        scratch_shapes=[pltpu.SemaphoreType.DMA(())] * 2,
        compiler_params=params_of(2),
    )(both)


def masked_pairs(source, target, pairs, scale):
    rows = source.shape[0]
    low_lanes = lax.broadcasted_iota(jnp.int32, (rows, PAIR), 1) < HD
    for p in range(pairs):
        both = source[:, p * PAIR : (p + 1) * PAIR]
        if scale is not None:
            both = both * jnp.asarray(scale, both.dtype)
        zero = jnp.zeros_like(both)
        target[p, :rows, :] = jnp.where(low_lanes, both, zero)
        target[p, rows:, :] = jnp.where(low_lanes, zero, both)


def tile_bias(j, q_first, row_info, key_info, bias):
    seg_q, bits_q = row_info[0:1, :], row_info[1:2, :]
    queries = bias.shape[1]
    for part in range(KT // HD):
        block = j * (KT // HD) + part
        bit = jnp.bitwise_and(
            lax.shift_right_logical(bits_q, jnp.full_like(bits_q, block)), 1
        )
        wanted = jnp.where(bit == 1, seg_q, -1)
        base = pl.multiple_of(j * KT + part * HD, HD)
        seg_k = key_info[pl.ds(base, HD), :]
        key_at = base + lax.broadcasted_iota(jnp.int32, (HD, queries), 0)
        query_at = q_first + lax.broadcasted_iota(jnp.int32, (HD, queries), 1)
        allowed = (seg_k == wanted) | (key_at == query_at)
        bias[part * HD : (part + 1) * HD, :] = jnp.where(allowed, 0.0, NEGATIVE)


def attend_forward_kernel(
    bounds, q_ref, kv_ref, row_info, key_info, out_ref, log_ref, q_pairs, v_turned, bias, top, total, acc
):
    step = pl.program_id(0)
    rows, width = q_ref.shape
    pairs = width // PAIR
    tiles = kv_ref.shape[0] // KT

    @pl.when(step == 0)
    def _():
        for j in range(tiles):
            v_turned[j] = kv_ref[j * KT : (j + 1) * KT, width:].T

    masked_pairs(q_ref, q_pairs, pairs, HD**-0.5)
    top[...] = jnp.full_like(top, NEGATIVE)
    total[...] = jnp.zeros_like(total)
    acc[...] = jnp.zeros_like(acc)
    q_first = bounds[step, 2]

    @pl.loop(bounds[step, 0], bounds[step, 1])
    def _(j):
        tile_bias(j, q_first, row_info, key_info, bias)
        keys_at = pl.multiple_of(j * KT, KT)
        for p in range(pairs):
            keys = kv_ref[pl.ds(keys_at, KT), p * PAIR : (p + 1) * PAIR]
            scores = nt(keys, q_pairs[p])
            for e in range(2):
                h = 2 * p + e
                mine = scores[:, e * rows : (e + 1) * rows] + bias[...]
                before = top[h : h + 1, :]
                now = jnp.maximum(before, jnp.max(mine, axis=0, keepdims=True))
                fade = jnp.exp(before - now)
                expos = jnp.exp(mine - now)
                top[h : h + 1, :] = now
                total[h : h + 1, :] = fade * total[h : h + 1, :] + jnp.sum(
                    expos, axis=0, keepdims=True
                )
                span = slice(h * HD, (h + 1) * HD)
                acc[span, :] = acc[span, :] * fade + nn(v_turned[j, span, :], expos.astype(BF))

    heads = width // HD
    for h in range(heads):
        span = slice(h * HD, (h + 1) * HD)
        acc[span, :] = acc[span, :] / total[h : h + 1, :]
    out_ref[...] = acc[...].T.astype(BF)
    log_ref[...] = top[...] + jnp.log(jnp.maximum(total[...], 1e-37))


def attend_forward(bounds, qkv, kv, row_info, key_info):
    rows, width = qkv.shape[0], qkv.shape[1] // 3
    keys = kv.shape[0]
    stat_rows = 16
    return pl.pallas_call(
        attend_forward_kernel,
        name="attend_forward",
        grid_spec=pltpu.PrefetchScalarGridSpec(
            num_scalar_prefetch=1,
            grid=(rows // QT,),
            in_specs=[
                pl.BlockSpec((QT, width), lambda i, b: (i, 0)),
                pl.BlockSpec((keys, 2 * width), lambda i, b: (0, 0), pipeline_mode=pl.Buffered(1)),
                pl.BlockSpec((8, QT), lambda i, b: (0, i)),
                pl.BlockSpec((keys, 1), lambda i, b: (0, 0), pipeline_mode=pl.Buffered(1)),
            ],
            out_specs=[
                pl.BlockSpec((QT, width), lambda i, b: (i, 0)),
                pl.BlockSpec((stat_rows, QT), lambda i, b: (0, i)),
            ],
            scratch_shapes=[
                pltpu.VMEM((width // PAIR, 2 * QT, PAIR), BF),
                pltpu.VMEM((keys // KT, width, KT), BF),
                pltpu.VMEM((KT, QT), F32),
                pltpu.VMEM((stat_rows, QT), F32),
                pltpu.VMEM((stat_rows, QT), F32),
                pltpu.VMEM((width, QT), F32),
            ],
        ),
        out_shape=[
            jax.ShapeDtypeStruct((rows, width), BF),
            jax.ShapeDtypeStruct((stat_rows, rows), F32),
        ],
        compiler_params=params_of(),
    )(bounds, qkv, kv, row_info, key_info)


def attend_backward_kernel(
    bounds, q_ref, kv_ref, row_info, key_info, out_ref, log_ref, grad_ref,
    dq_ref, dkv_ref, q_pairs, g_pairs, k_turned, bias, inner, dq_acc, dkv_acc,
):
    step = pl.program_id(0)
    rows, width = q_ref.shape
    pairs = width // PAIR
    tiles = kv_ref.shape[0] // KT

    @pl.when(step == 0)
    def _():
        for j in range(tiles):
            k_turned[j] = kv_ref[j * KT : (j + 1) * KT, :width].T
        dkv_acc[...] = jnp.zeros_like(dkv_acc)

    masked_pairs(q_ref, q_pairs, pairs, HD**-0.5)
    masked_pairs(grad_ref, g_pairs, pairs, None)
    head_of = lax.broadcasted_iota(jnp.int32, (inner.shape[0], width), 1) // HD
    row_of = lax.broadcasted_iota(jnp.int32, (inner.shape[0], width), 0)
    chosen = jnp.where(head_of == row_of, 1.0, 0.0)
    product = out_ref[...].astype(F32) * grad_ref[...].astype(F32)
    inner[...] = nt(chosen, product, precision=lax.Precision.HIGHEST)
    dq_acc[...] = jnp.zeros_like(dq_acc)
    q_first = bounds[step, 2]

    @pl.loop(bounds[step, 0], bounds[step, 1])
    def _(j):
        tile_bias(j, q_first, row_info, key_info, bias)
        here = pl.ds(pl.multiple_of(j * KT, KT), KT)
        for p in range(pairs):
            lanes = slice(p * PAIR, (p + 1) * PAIR)
            v_lanes = slice(width + p * PAIR, width + (p + 1) * PAIR)
            scores = nt(kv_ref[here, lanes], q_pairs[p])
            grad_probs = nt(kv_ref[here, v_lanes], g_pairs[p])
            probs, grads = [], []
            for e in range(2):
                h = 2 * p + e
                cols = slice(e * rows, (e + 1) * rows)
                prob = jnp.exp(scores[:, cols] + bias[...] - log_ref[h : h + 1, :])
                grad = (prob * (grad_probs[:, cols] - inner[h : h + 1, :])).astype(BF)
                probs.append(prob.astype(BF))
                grads.append(grad)
                span = slice(h * HD, (h + 1) * HD)
                dq_acc[span, :] += nn(k_turned[j, span, :], grad)
            dkv_acc[here, lanes] += nn(jnp.concatenate(grads, axis=1), q_pairs[p])
            dkv_acc[here, v_lanes] += nn(jnp.concatenate(probs, axis=1), g_pairs[p])

    dq_ref[...] = (dq_acc[...] * HD**-0.5).T.astype(BF)

    @pl.when(step == pl.num_programs(0) - 1)
    def _():
        dkv_ref[...] = dkv_acc[...].astype(BF)


def attend_backward(bounds, qkv, kv, row_info, key_info, attn, logs, grad_attn):
    rows, width = attn.shape
    keys = kv.shape[0]
    stat_rows = logs.shape[0]
    whole = dict(pipeline_mode=pl.Buffered(1))
    return pl.pallas_call(
        attend_backward_kernel,
        name="attend_backward",
        grid_spec=pltpu.PrefetchScalarGridSpec(
            num_scalar_prefetch=1,
            grid=(rows // QT,),
            in_specs=[
                pl.BlockSpec((QT, width), lambda i, b: (i, 0)),
                pl.BlockSpec((keys, 2 * width), lambda i, b: (0, 0), **whole),
                pl.BlockSpec((8, QT), lambda i, b: (0, i)),
                pl.BlockSpec((keys, 1), lambda i, b: (0, 0), **whole),
                pl.BlockSpec((QT, width), lambda i, b: (i, 0)),
                pl.BlockSpec((stat_rows, QT), lambda i, b: (0, i)),
                pl.BlockSpec((QT, width), lambda i, b: (i, 0)),
            ],
            out_specs=[
                pl.BlockSpec((QT, width), lambda i, b: (i, 0)),
                pl.BlockSpec((keys, 2 * width), lambda i, b: (0, 0), **whole),
            ],
            scratch_shapes=[
                pltpu.VMEM((width // PAIR, 2 * QT, PAIR), BF),
                pltpu.VMEM((width // PAIR, 2 * QT, PAIR), BF),
                pltpu.VMEM((keys // KT, width, KT), BF),
                pltpu.VMEM((KT, QT), F32),
                pltpu.VMEM((stat_rows, QT), F32),
                pltpu.VMEM((width, QT), F32),
                pltpu.VMEM((keys, 2 * width), F32),
            ],
        ),
        out_shape=[
            jax.ShapeDtypeStruct((rows, width), BF),
            jax.ShapeDtypeStruct((keys, 2 * width), BF),
        ],
        compiler_params=params_of(),
    )(bounds, qkv, kv, row_info, key_info, attn, logs, grad_attn)


def attention_plan(segment_ids, pad_mask, random_blocks, global_blocks, rows):
    seq_count, nblocks = random_blocks.shape[0], random_blocks.shape[1]
    seq_len = segment_ids.shape[0] // seq_count
    rank = lax.axis_index("tensor")
    seq, half = rank // 2, lax.rem(rank, 2)
    segs = lax.dynamic_index_in_dim(segment_ids.reshape(seq_count, seq_len), seq, 0, False)
    pads = lax.dynamic_index_in_dim(pad_mask.reshape(seq_count, seq_len), seq, 0, False)
    randoms = lax.dynamic_index_in_dim(random_blocks, seq, 0, False)
    globs = lax.dynamic_index_in_dim(global_blocks, seq, 0, False)
    block_size = seq_len // nblocks
    one = jnp.int32(1)
    block = jnp.arange(nblocks, dtype=jnp.int32)

    def either(a, b):
        return jnp.bitwise_or(a, b)

    block_bits = lax.shift_left(one, block)
    window = either(
        block_bits,
        either(
            jnp.where(block > 0, lax.shift_left(one, jnp.maximum(block - 1, 0)), 0),
            jnp.where(
                block < nblocks - 1, lax.shift_left(one, jnp.minimum(block + 1, nblocks - 1)), 0
            ),
        ),
    )
    for r in range(randoms.shape[1]):
        window = either(window, lax.shift_left(one, randoms[:, r]))
    glob_bits = either(lax.shift_left(one, globs[:, 0]), lax.shift_left(one, globs[:, 1]))
    first = half * rows
    seg_q = lax.dynamic_slice_in_dim(segs, first, rows)
    own_bits = lax.dynamic_slice_in_dim(window, half * (rows // block_size), rows // block_size)
    bits = jnp.broadcast_to(own_bits[:, None], (rows // block_size, block_size)).reshape(rows)
    numbers = jnp.arange(globs.shape[0], dtype=jnp.int32)
    is_doc = seg_q[None, :] == numbers[:, None]
    bits = either(bits, jnp.sum(jnp.where(is_doc, glob_bits[:, None], 0), axis=0))
    row_info = jnp.concatenate(
        [seg_q[None], bits[None], jnp.zeros((6, rows), jnp.int32)], axis=0
    )
    key_info = jnp.where(pads == 1, segs, -2)[:, None]
    tiles = seg_q.reshape(rows // QT, QT)
    low = jnp.sum((segs[None, :] < tiles[:, :1]).astype(jnp.int32), axis=1)
    high = jnp.sum((segs[None, :] <= tiles[:, -1:]).astype(jnp.int32), axis=1)
    starts = first + QT * jnp.arange(rows // QT, dtype=jnp.int32)
    bounds = jnp.stack([low // KT, (high + KT - 1) // KT, starts, starts], axis=1)
    return bounds, row_info, key_info


def normalize(resid):
    center = resid - jnp.mean(resid, axis=1, keepdims=True)
    inverse = lax.rsqrt(jnp.mean(center * center, axis=1, keepdims=True) + EPSILON)
    return center * inverse, inverse


def norm_backward(grad_normed, normal_hat, inverse, gain):
    grad_hat = grad_normed * gain
    grad_resid = inverse * (
        grad_hat
        - jnp.mean(grad_hat, axis=1, keepdims=True)
        - normal_hat * jnp.mean(grad_hat * normal_hat, axis=1, keepdims=True)
    )
    return grad_resid, jnp.sum(grad_normed * normal_hat, axis=0), jnp.sum(grad_normed, axis=0)


def on_device(
    layer_in, query_weight, key_weight, value_weight, output_weight, inner_weight, outer_weight,
    query_bias, value_bias, output_bias, inner_bias, outer_bias, first_gain, first_shift,
    second_gain, second_shift, segment_ids, pad_mask, random_blocks, global_blocks, output_grad,
):
    rows, width = layer_in.shape
    dp, tp = lax.axis_size("dp"), lax.axis_size("tensor")
    own_rows, own_cols = query_weight.shape
    own_units = inner_weight.shape[1]
    units = own_units * tp

    packed = jnp.concatenate(
        [query_weight, key_weight, value_weight, output_weight.T, inner_weight, outer_weight.T],
        axis=1,
    )
    every = lax.all_gather(packed, ("dp", "tensor"), axis=0, tiled=False)
    every = every.reshape(dp, tp, own_rows, packed.shape[1])

    def whole(first, wide):
        part = every[:, :, :, first : first + wide]
        return part.transpose(0, 2, 1, 3).reshape(dp * own_rows, tp * wide)

    wqkv = jnp.concatenate([whole(i * own_cols, own_cols) for i in range(3)], axis=1)
    wo_t = whole(3 * own_cols, own_cols)
    w_in = whole(4 * own_cols, own_units)
    w_out_t = whole(4 * own_cols + own_units, own_units)

    small = [query_bias, value_bias, output_bias, outer_bias, first_gain, first_shift,
             second_gain, second_shift, inner_bias]
    sizes = [s.shape[0] for s in small]
    all_small = lax.all_gather(jnp.concatenate(small), ("dp", "tensor"), axis=0, tiled=False)
    offsets = [sum(sizes[:i]) for i in range(len(sizes))]
    (bq, bv, bo, bout, g1, s1, g2, s2, bin_) = (
        all_small[:, o : o + n].reshape(-1) for o, n in zip(offsets, sizes)
    )
    bqkv = jnp.concatenate([bq, jnp.zeros_like(bq), bv])

    bounds, row_info, key_info = attention_plan(
        segment_ids, pad_mask, random_blocks, global_blocks, rows
    )
    qkv = (nn(layer_in, wqkv) + bqkv).astype(BF)
    kv = gather_pair(qkv, width).reshape(2 * rows, 2 * width)
    attn, logs = attend_forward(bounds, qkv, kv, row_info, key_info)

    first_resid = layer_in.astype(F32) + nt(attn, wo_t) + bo
    first_hat, first_inverse = normalize(first_resid)
    first_norm = first_hat * g1 + s1
    norm_low = first_norm.astype(BF)
    inner_pre = nn(norm_low, w_in) + bin_
    inner_act, gelu_pull = jax.vjp(partial(jax.nn.gelu, approximate=False), inner_pre)
    hidden = inner_act.astype(BF)
    second_resid = first_norm + nt(hidden, w_out_t) + bout
    second_hat, second_inverse = normalize(second_resid)
    layer_out = (second_hat * g2 + s2).astype(BF)

    grad_second, d_g2, d_s2 = norm_backward(output_grad.astype(F32), second_hat, second_inverse, g2)
    d_bout = jnp.sum(grad_second, axis=0)
    grad_ffn = grad_second.astype(BF)
    d_w_out_t = tn(grad_ffn, hidden)
    grad_inner = gelu_pull(nn(grad_ffn, w_out_t))[0].astype(BF)
    d_bin = jnp.sum(grad_inner.astype(F32), axis=0)
    d_w_in = tn(norm_low, grad_inner)
    grad_first_norm = grad_second + nt(grad_inner, w_in)
    grad_first, d_g1, d_s1 = norm_backward(grad_first_norm, first_hat, first_inverse, g1)
    d_bo = jnp.sum(grad_first, axis=0)
    grad_proj = grad_first.astype(BF)
    d_wo_t = tn(grad_proj, attn)
    grad_attn = nn(grad_proj, wo_t).astype(BF)

    dq, dkv = attend_backward(bounds, qkv, kv, row_info, key_info, attn, logs, grad_attn)
    both = dkv.reshape(2, rows, 2 * width)
    half = lax.rem(lax.axis_index("tensor"), 2)
    other = swap_pair(both)
    mine = lax.dynamic_index_in_dim(both, half, 0, False)
    dkv_own = (mine.astype(F32) + other.astype(F32)).astype(BF)
    d_qkv = jnp.concatenate([dq, dkv_own], axis=1)
    d_bqkv = jnp.sum(d_qkv.astype(F32), axis=0)
    d_wqkv = tn(layer_in, d_qkv)
    input_grad = grad_first + nt(d_qkv, wqkv)

    def split(full, wide):
        return full.reshape(dp, own_rows, tp, wide).transpose(0, 2, 1, 3).astype(BF)

    grads = jnp.concatenate(
        [split(d_wqkv[:, i * width : (i + 1) * width], own_cols) for i in range(3)]
        + [split(d_wo_t, own_cols), split(d_w_in, own_units), split(d_w_out_t, own_units)],
        axis=3,
    ).reshape(dp * tp * own_rows, packed.shape[1])
    mine_w = lax.psum_scatter(grads, ("dp", "tensor"), scatter_dimension=0, tiled=True).astype(F32)
    small_grads = [d_bqkv[:width], d_bqkv[2 * width :], d_bo, d_bout, d_g1, d_s1, d_g2, d_s2, d_bin]
    small_flat = jnp.concatenate([g.reshape(dp * tp, -1) for g in small_grads], axis=1)
    mine_s = lax.psum_scatter(small_flat, ("dp", "tensor"), scatter_dimension=0, tiled=True)[0]
    (r_bq, r_bv, r_bo, r_bout, r_g1, r_s1, r_g2, r_s2, r_bin) = (
        mine_s[o : o + n] for o, n in zip(offsets, sizes)
    )
    c = own_cols
    return (
        layer_out,
        input_grad,
        mine_w[:, :c],
        mine_w[:, c : 2 * c],
        mine_w[:, 2 * c : 3 * c],
        mine_w[:, 3 * c : 4 * c].T,
        mine_w[:, 4 * c : 4 * c + own_units],
        mine_w[:, 4 * c + own_units :].T,
        r_bq, r_bv, r_bo, r_bin, r_bout, r_g1, r_s1, r_g2, r_s2,
    )


def solution(mesh):
    tokens = P(("dp", "tensor"), None)
    vector = P(("dp", "tensor"))
    cols, turned = P("dp", "tensor"), P("tensor", "dp")
    return jax.shard_map(
        on_device,
        mesh=mesh,
        in_specs=(tokens, cols, cols, cols, turned, cols, turned)
        + (vector,) * 9
        + (P("dp"), P("dp"), P("dp", None, None), P("dp", None, None), tokens),
        out_specs=(tokens, tokens, cols, cols, cols, turned, cols, turned) + (vector,) * 9,
        check_vma=False,
    )
```

time: 2200 us -> 790 us (0.36)
  waiting for transfers between devices: 658 us -> 149 us
  other arithmetic: 397 us -> 15.7 us
  local copies, waits for them, and re-layouts: 487 us -> 185 us
  matrix products: 410 us -> 126 us
  Pallas kernels: 0 us -> 198 us
  blocking collectives: 211 us -> 89.5 us
    reduce_scatter x6 -> x1, waiting for transfers between devices: 312 us -> 95.9 us  [on_device(): lax.psum_scatter(grads, ('dp', 'tensor'), scatter_dimension=0, tiled=True)]
    scatter-add x4 -> x0, other arithmetic: 204 us -> none  [the longest x2 102 us: attend_backward(): grad_key = empty.at[gather_ids].add(key_parts)]
    unnamed x20 -> x2, waiting for transfers between devices: 199 us -> 0.03 us
    pallas_call x0 -> x4, Pallas kernels: none -> 198 us  [the longest x1 96.7 us: gather_pair(): pl.pallas_call(partial(gather_pair_kernel, first), name='gather_pair', ou...]
    gather x19 -> x0, local copies, waits for them, and re-layouts: 194 us -> none  [the longest x8 105 us: block_operands(): key_blocks = keys.reshape(key_count, block_size, heads_here, HD)[gather_ids]]
    dot_general x25 -> x12, matrix products: 308 us -> 126 us  [the longest x4 75.6 us: nn(): lax.dot_general(left, right, (((1,), (0,)), ((), ())), preferred_element_...]
    all_gather x4 -> x0, blocking collectives: 126 us -> none  [the longest x1 33 us: on_device(): lax.all_gather(output_weight, 'dp', axis=1, tiled=True)]
    while x6 -> x0, matrix products: 95.2 us -> none
  transfers between devices with their start and end apart: 16 -> 2, of which waited for: 12 -> 2; matrix products, arithmetic and copies ran while one was open for 8% -> 5% of each run, Pallas kernels for 0% -> 0%
where the time goes in v1:
time: 790 us; the launch traced here: 778 us
  Pallas kernels  198 us (25%)
  local copies, waits for them, and re-layouts  185 us (23%)
  waiting for transfers between devices  149 us (19%)
  matrix products  126 us (16%)
  blocking collectives  89.5 us (11%)
  other arithmetic  15.7 us (2%)
  between operations  15.2 us (2%)
    pallas_call x1, Pallas kernels, gather_pair(): pl.pallas_call(partial(gather_pair_kernel, first), name='gather_pair', ou...  96.7 us
    reduce_scatter x1, waiting for transfers between devices, on_device(): lax.psum_scatter(grads, ('dp', 'tensor'), scatter_dimension=0, tiled=True)  95.9 us
    unnamed x2, blocking collectives  89.5 us
    dot_general x4, matrix products, nn(): lax.dot_general(left, right, (((1,), (0,)), ((), ())), preferred_element_...  75.6 us
    concatenate x2, local copies, waits for them, and re-layouts, on_device(): jnp.concatenate([split(d_wqkv[:, i * width:(i + 1) * width], own_cols) fo...  53.5 us
    all_gather x1, waiting for transfers between devices, on_device(): every = lax.all_gather(packed, ('dp', 'tensor'), axis=0, tiled=False)  52.7 us
    pallas_call x1, Pallas kernels, attend_backward(): pl.pallas_call(attend_backward_kernel, name='attend_backward', grid_spec=...  47.8 us
    convert_element_type x9, local copies, waits for them, and re-layouts, split(): return full.reshape(dp, own_rows, tp, wide).transpose(0, 2, 1, 3).astype(BF)  47.5 us
  transfers between devices with their start and end apart: 2, of which 2 were waited for; matrix products, arithmetic and copies ran while one was open for 5% of the time, Pallas kernels for 0%

profile of v1, /device:TPU:0, one launch (start us, length us, event | category | flops | bytes accessed | tf_op | source)
XLA Modules:
  0.0 778.2 jit_solution(16178363098156893146)
XLA Ops:
  7.3 1.0 copy.159
  8.3 2.1 concatenate.24
  14.2 0.9 concatenate.26
  15.3 42.8 %all-reduce = f32[9216]{0:T(1024)S(1)} all-reduce(f32[9216]{0:T(1024)S(1)} %dynamic-update-slice), channel_id=3, replica_groups=mesh['dp'=8,'tensor'=4] {'dp','tensor'}, use_global_device_ids=true, to_apply=%add | all-reduce | flops 9216 | bytes 73728
  59.7 1.4 copy.164.key_info
  61.1 1.6 copy.169
  62.7 1.6 copy.150
  65.8 52.7 %all-gather.4.cloned.1.call-done = bf16[3072,2304]{1,0:T(8,128)(2,1)} async-done(((bf16[96,2304]{1,0:T(8,128)(2,1)}), bf16[3072,2304]{1,0:T(8,128)(2,1)}) %all-gather.4.cloned.1.call-update) | async-done | bytes 14155792 | tf_op jit(solution)/shard_map/all_gather | solution.py:395
  118.5 6.8 fusion.48
  125.3 6.7 fusion.47
  132.1 3.6 copy.190
  135.7 3.3 copy.192
  139.0 2.8 copy.188
  141.8 3.8 reshape.368
  145.6 2.8 copy.187
  148.4 3.8 reshape.362
  152.2 2.0 copy.186
  154.2 3.8 reshape.361
  158.0 1.0 copy.185
  159.0 1.3 reshape.360
  160.5 6.0 copy.189
  166.5 1.0 copy.191
  167.8 2.0 copy-done.8
  169.9 1.8 copy-done.20
  171.7 5.5 fusion.7.qkv_ref.q_ref
  177.2 96.7 %gather_pair.1 = bf16[2,1024,1536]{2,1,0:T(8,128)(2,1)} custom-call(bf16[1024,2304]{1,0:T(8,128)(2,1)} %fusion.7.qkv_ref.q_ref), custom_call_target="tpu_custom_call" | custom-call | tf_op jit(solution)/shard_map/gather_pair/pallas_call | solution.py:72
  273.9 36.5 %attend_forward.1 = (bf16[1024,768]{1,0:T(8,128)(2,1)}, f32[16,1024]{1,0:T(8,128)}) custom-call(s32[4,4]{1,0:T(4,128)} %pad_add_fusion.bounds, bf16[1024,2304]{1,0:T(8,128)(2,1)} %fusion.7.qkv_ref.q_ref, bf16[2048,1536]{1,0:T(8,128)(2,1)} %bitcast.113, s32[8,1024]{1,0:T(8,128)} %add_add_fusion.2.row_info, s32[2048,1]{1,0:T(8,128)} %copy.164.key_info), custom_call_target="tpu_custom_call" | custom-call | tf_op jit(solution)/shard_map/attend_forward/pallas_call | solution.py:187
  310.4 3.3 fusion.53
  314.1 48.9 %multiply_convert_fusion = (bf16[1024,3072]{1,0:T(8,128)(2,1)S(1)}, f32[1024,3072]{1,0:T(8,128)}, f32[1024,3072]{1,0:T(8,128)}) fusion(f32[3072]{0:T(1024)S(1)} %add.178, bf16[768,3072]{1,0:T(8,128)(2,1)S(1)} %bitcast.135, f32[1024,768]{0,1:T(8,128)S(1)} %get-tuple-element.163, f32[768]{0:T(1024)S(1)} %add.175, f32[768]{0:T(1024)S(1)} %mul.146, ...), kind=kOutput, calls=%fused_computation.4 | convolution fusion | flops 5043388416 | bytes 39348224 | tf_op jit(solution)/shard_map/dot_general | solution.py:37
  363.1 5.3 fusion.54
  368.8 1.0 copy-done.2
  370.6 7.4 convolution_convert_fusion
  378.1 18.6 %convert_reduce_fusion = (f32[3072]{0:T(1024)S(1)}, bf16[1024,3072]{1,0:T(8,128)(2,1)}) fusion(f32[1024,3072]{1,0:T(8,128)} %get-tuple-element.126, bf16[768,3072]{1,0:T(8,128)(2,1)} %bitcast.131, f32[1024]{0:T(1024)S(1)} %broadcast_multiply_fusion.2, f32[1024,768]{0,1:T(8,128)S(1)} %get-tuple-element.166, f32[1024]{0:T(1024)S(1)} %broadcast_multiply_fusion.4, ...), kind=kOutput, calls=%fused_computation.2 | convolution fusion | flops 4892390400 | bytes 40938496 | tf_op jit(solution)/shard_map/dot_general | solution.py:37
  396.7 10.9 %multiply_reduce_fusion = (f32[768]{0:T(1024)S(1)}, f32[1024]{0:T(1024)S(1)}, f32[1024]{0:T(1024)S(1)}, f32[768]{0:T(1024)S(1)}, f32[1024,768]{0,1:T(8,128)S(1)}) fusion(f32[1024,768]{0,1:T(8,128)} %copy-done.3, f32[1024]{0:T(1024)S(1)} %add_rsqrt_fusion.1, f32[1024]{0:T(1024)S(1)} %broadcast_multiply_fusion.5, f32[768]{0:T(1024)S(1)} %mul.146, ...), kind=kOutput, calls=%fused_computation.38 | convolution fusion | flops 4845989888 | bytes 22065152 | tf_op jit(solution)/shard_map/dot_general | solution.py:31
  407.6 7.2 convolution_convert_fusion.1
  414.9 1.1 fusion.44
  416.1 2.6 convolution_convert_fusion.3.grad_ref
  418.7 2.5 convolution_convert_fusion.4
  421.2 9.8 %convert_element_type.137 = bf16[8,96,4,768]{3,2,1,0:T(4,128)(2,1)} reshape(bf16[768,3072]{1,0:T(8,128)(2,1)} %convolution_convert_fusion) | data formatting | bytes 9437184 | tf_op jit(solution)/shard_map/convert_element_type | solution.py:461
  430.9 9.8 %convert_element_type.134 = bf16[8,96,4,768]{3,2,1,0:T(4,128)(2,1)} reshape(bf16[768,3072]{1,0:T(8,128)(2,1)} %convolution_convert_fusion.1) | data formatting | bytes 9437184 | tf_op jit(solution)/shard_map/convert_element_type | solution.py:461
  440.7 4.4 convert_element_type.131
  445.1 47.8 %attend_backward.1 = (bf16[1024,768]{1,0:T(8,128)(2,1)}, bf16[2048,1536]{1,0:T(8,128)(2,1)}) custom-call(s32[4,4]{1,0:T(4,128)} %pad_add_fusion.bounds, bf16[1024,2304]{1,0:T(8,128)(2,1)} %fusion.7.qkv_ref.q_ref, bf16[2048,1536]{1,0:T(8,128)(2,1)} %bitcast.114, s32[8,1024]{1,0:T(8,128)} %add_add_fusion.2.row_info, s32[2048,1]{1,0:T(8,128)} %copy.164.key_info, ...), custom_call_target="tpu_custom_call" | custom-call | tf_op jit(solution)/shard_map/attend_backward/pallas_call | solution.py:279
  493.0 16.9 %swap_pair.1 = bf16[1024,1536]{1,0:T(8,128)(2,1)} custom-call(bf16[2,1024,1536]{2,1,0:T(8,128)(2,1)} %bitcast.121), custom_call_target="tpu_custom_call" | custom-call | tf_op jit(solution)/shard_map/swap_pair/pallas_call | solution.py:95
  509.9 3.8 fusion.6
  513.8 4.5 fusion.8
  518.2 1.9 fusion.49
  520.1 4.0 convert_element_type.128
  524.1 3.8 copy.175
  527.9 4.0 convert_element_type.126
  531.9 4.1 copy.174
  536.0 4.0 convert_element_type.124
  540.0 3.8 copy.173
  543.8 42.3 %concatenate.30 = bf16[8,4,96,2304]{3,1,2,0:T(4,128)(2,1)} concatenate(bf16[8,4,96,192]{3,1,2,0:T(4,128)(2,1)} %copy.173, bf16[8,4,96,192]{3,1,2,0:T(4,128)(2,1)} %copy.174, bf16[8,4,96,192]{3,1,2,0:T(4,128)(2,1)} %copy.175, bf16[8,4,96,192]{3,1,2,0:T(4,128)(2,1)} %bitcast.123, bf16[8,4,96,768]{3,1,2,0:T(4,128)(2,1)} %bitcast.116, bf16[8,4,96,768]{3,1,2,0:T(4,128)(2,1)} %bitcast.115), dimensions={3} | concatenate | bytes 28311552 | tf_op jit(solution)/shard_map/concatenate | solution.py:463
  586.0 11.2 %copy.176 = bf16[8,4,96,2304]{3,2,1,0:T(8,128)(2,1)} copy(bf16[8,4,96,2304]{3,1,2,0:T(4,128)(2,1)} %concatenate.30) | data formatting | bytes 28311552 | tf_op jit(solution)/shard_map/concatenate | solution.py:463
  598.3 4.2 fusion.15
  602.8 2.8 copy.177
  605.6 9.3 %convolution_add_fusion.1 = f32[1024,768]{0,1:T(8,128)} fusion(f32[1024,768]{0,1:T(8,128)} %copy-done.10, bf16[768,2304]{0,1:T(8,128)(2,1)} %copy-done.20, bf16[1024,1536]{1,0:T(8,128)(2,1)S(1)} %copy-done.6, bf16[1024,768]{1,0:T(8,128)(2,1)} %get-tuple-element.23), kind=kOutput, calls=%fused_computation.52 | convolution fusion | flops 3634102272 | bytes 14548992 | tf_op jit(solution)/shard_map/dot_general | solution.py:31
  614.9 3.7 copy.178
  618.6 2.2 convert_reduce_fusion.1
  621.1 46.7 %all-reduce.1 = f32[32,288]{1,0:T(8,128)S(1)} all-reduce(f32[32,288]{1,0:T(8,128)S(1)} %concatenate.31), channel_id=5, replica_groups=mesh['dp'=8,'tensor'=4] {'dp','tensor'}, use_global_device_ids=true, to_apply=%region_20.21.clone | all-reduce | flops 9216 | bytes 73728
  669.0 95.9 %reduce-scatter.2.cloned.1.call-done = bf16[96,2304]{1,0:T(8,128)(2,1)} async-done(((bf16[3072,2304]{1,0:T(8,128)(2,1)}), bf16[96,2304]{1,0:T(8,128)(2,1)}) %reduce-scatter.2.cloned.1.call-update) | async-done | bytes 442384 | tf_op jit(solution)/shard_map/reduce_scatter | solution.py:468
  765.0 1.1 convert_element_type.139
  767.6 1.6 slice.247
  769.3 1.6 fusion.50
  (127 shorter events, 13.6 us)
Async XLA Ops:
  7.2 3.3 copy-start
  7.2 53.9 %copy-start.12 = (bf16[1024,768]{1,0:T(8,128)(2,1)S(1)}, bf16[1024,768]{1,0:T(8,128)(2,1)}, u32[]{:S(2)}) copy-start(bf16[1024,768]{1,0:T(8,128)(2,1)} %param.41) | copy-start | bytes 4718596
  7.2 111.3 %all-gather.4.cloned.1.call-start = ((), (), s32[]{:S(2)}) async-start(), calls=%async_computation.2 | async-start | bytes 14598144 | tf_op jit(solution)/shard_map/all_gather | solution.py:395
  8.3 54.4 %copy-start.13 = (bf16[1024,768]{1,0:T(8,128)(2,1)S(1)}, bf16[1024,768]{1,0:T(8,128)(2,1)}, u32[]{:S(2)}) copy-start(bf16[1024,768]{1,0:T(8,128)(2,1)} %param.21) | copy-start | bytes 4718596
  10.4 754.6 %reduce-scatter.2.cloned.1.call-start = ((), (), s32[]{:S(2)}) async-start(), calls=%async_computation.1 | async-start | bytes 14598144 | tf_op jit(solution)/shard_map/reduce_scatter | solution.py:468
  61.1 3.3 copy-start.22
  166.5 1.3 copy-start.9
  167.7 146.4 %copy-start.7 = (bf16[96,8,4,768]{3,1,2,0:T(8,128)(2,1)}, bf16[96,8,4,768]{3,1,2,0:T(8,128)(2,1)S(1)}, u32[]{:S(2)}) copy-start(bf16[96,8,4,768]{3,1,2,0:T(8,128)(2,1)S(1)} %copy.191) | copy-start | bytes 14155780
  167.7 2.1 copy-start.8
  167.7 4.0 copy-start.14
  169.9 1.8 copy-start.20
  273.9 36.5 %copy-start.16 = (bf16[1024,768]{0,1:T(8,128)(2,1)S(1)}, bf16[1024,768]{0,1:T(8,128)(2,1)}, u32[]{:S(2)}) copy-start(bf16[1024,768]{0,1:T(8,128)(2,1)} %copy.150) | copy-start | bytes 4718596
  273.9 36.5 %copy-start.18 = (bf16[768,768]{0,1:T(8,128)(2,1)S(1)}, bf16[768,768]{0,1:T(8,128)(2,1)}, u32[]{:S(2)}) copy-start(bf16[768,768]{0,1:T(8,128)(2,1)} %reshape.368) | copy-start | bytes 3538948
  310.4 52.6 %slice-start = ((s8[4718592]{0:T(1024)(128)(4,1)}), s8[4194304]{0:T(1024)(128)(4,1)S(1)}, s32[]{:S(2)}) async-start(s8[4718592]{0:T(1024)(128)(4,1)} %bitcast.132), calls=%async_computation.3 | async-start | bytes 8388608
  313.7 49.3 %copy-start.3 = (f32[1024,768]{0,1:T(8,128)}, f32[1024,768]{0,1:T(8,128)S(1)}, u32[]{:S(2)}) copy-start(f32[1024,768]{0,1:T(8,128)S(1)} %get-tuple-element.163) | copy-start | bytes 9437188
  314.1 48.9 %slice-start.1 = ((s8[4718592]{0:T(1024)(128)(4,1)}), s8[524288]{0:T(1024)(128)(4,1)S(1)}, s32[]{:S(2)}) async-start(s8[4718592]{0:T(1024)(128)(4,1)} %bitcast.132), calls=%async_computation.4 | async-start | bytes 1048576
  368.4 1.4 copy-start.2
  396.7 10.9 %copy-start.4 = (f32[1024,768]{0,1:T(8,128)S(1)}, f32[1024,768]{0,1:T(8,128)}, u32[]{:S(2)}) copy-start(f32[1024,768]{0,1:T(8,128)} %copy-done.3) | copy-start | bytes 9437188
  396.7 10.9 %copy-start.23 = (bf16[1024,3072]{1,0:T(8,128)(2,1)S(1)}, bf16[1024,3072]{1,0:T(8,128)(2,1)}, u32[]{:S(2)}) copy-start(bf16[1024,3072]{1,0:T(8,128)(2,1)} %get-tuple-element.169) | copy-start | bytes 18874372
  414.9 1.3 copy-start.19
  416.0 2.7 copy-start.10
  416.1 2.6 copy-start.11
  509.9 3.9 copy-start.15
  509.9 3.9 copy-start.17
  513.7 4.5 copy-start.5
  597.2 0.7 copy-start.21
  602.5 3.1 copy-start.6
  614.9 156.0 %copy-start.1 = (s32[2,32,3]{1,0,2:T(2,128)S(1)}, s32[2,32,3]{1,0,2:T(2,128)}, u32[]{:S(2)}) copy-start(s32[2,32,3]{1,0,2:T(2,128)} %param.39) | copy-start | bytes 2308
Sparse Core Ops, SparseCore 0:
  11.5 106.9 all-gather.3
  597.4 167.5 reduce-scatter.1
